TPU v7x, 1024 devices: a whole 4x8x16 slice. The times are simulated.
1024 devices in a mesh: member: 64 (over z, x), region: 16 (over y, core).
Axes of the slice: x: 4, y: 8, z: 16, core: 2. Of those that a mesh axis runs over, the one named last changes fastest.
Arguments:
- ensemble: bfloat16 [1024, 16, 64, 512], P('member', 'region'), may hold values from -6 to 6
- obs_store: bfloat16 [16, 64, 5, 128, 1024], P('region', 'member'), may hold values from -4 to 4
- block_ids: int32 [16, 64, 3], P('region', 'member'), may hold values from 0 to 4, as said below
- block_src: int32 [16, 64, 3], P('region', 'member'), may hold values from 0 to 2, as said below
- block_count: int32 [16, 64], P('region', 'member'), may hold values from 1 to 3, as said below
Outputs:
- analysis: bfloat16 [1024, 16, 64, 512], P('member', 'region')
Inputs may be any that keep to these rules, and one draw needn't show every extreme that they name: `block_ids`: within one patch's list the first 3 entries are distinct store indices. `block_src`: region 0 never names the region below and region 16 - 1 never names the region above. `block_count`: every region has a patch with 3 blocks.
All inputs are finite; a program needn't handle non-finite values.
Results may differ from a plain program's by a relative error of at most 0.0021.
Values may be sent and summed in bfloat16 or wider, within the bound.
A program may use at most 32 MiB of HBM per device.

v0:
```python
import jax
import jax.numpy as jnp
from jax import lax
from jax.sharding import PartitionSpec as P

K = 1024
OBS_DEV = 5
MAXB = 3


def padded(cells, sides, width):
    for axis, dim in sides:
        count = lax.axis_size(axis)
        ends = count - 1
        head = lax.slice_in_dim(cells, 0, width, axis=dim)
        tail = lax.slice_in_dim(cells, cells.shape[dim] - width, cells.shape[dim], axis=dim)
        cells = jnp.concatenate(
            [
                lax.ppermute(tail, axis, [(i, (i + 1) % count) for i in range(ends)]),
                cells,
                lax.ppermute(head, axis, [((i + 1) % count, i) for i in range(ends)]),
            ],
            axis=dim,
        )
    return cells


def transform(gram_matrix, slab_items):
    members = slab_items.reshape(slab_items.shape[0], slab_items.shape[3])
    first_term = jnp.dot(gram_matrix, members, preferred_element_type=jnp.float32).astype(
        jnp.bfloat16
    )
    second_term = jnp.dot(gram_matrix, first_term, preferred_element_type=jnp.float32)
    fresh = members.astype(jnp.float32) - first_term.astype(jnp.float32) + second_term
    return fresh.astype(jnp.bfloat16).reshape(slab_items.shape)


def shards(ensemble, obs_store, block_ids, block_src, block_count):
    own_ids = block_ids[0, 0]
    own_src = block_src[0, 0]
    rims = padded(obs_store, (("region", 0),), 1)
    pooled = rims.reshape(3 * OBS_DEV, rims.shape[3], rims.shape[4])
    chosen = jnp.take(pooled, own_src * OBS_DEV + own_ids, axis=0)
    live_slots = jnp.arange(MAXB, dtype=jnp.int32) < block_count[0, 0]
    chosen = jnp.where(live_slots[:, None, None], chosen, jnp.zeros((), chosen.dtype))
    stacked = chosen.reshape(-1, chosen.shape[2])
    gram_full = lax.dot_general(
        stacked, stacked, (((0,), (0,)), ((), ())), preferred_element_type=jnp.float32
    )
    gram_matrix = (gram_full / (2.0 * K)).astype(jnp.bfloat16)
    moved = transform(
        gram_matrix, lax.all_to_all(ensemble, "member", split_axis=2, concat_axis=0, tiled=True)
    )
    return lax.all_to_all(moved, "member", split_axis=0, concat_axis=2, tiled=True)


def solution(mesh):
    return jax.shard_map(
        shards,
        mesh=mesh,
        in_specs=(
            P("member", "region", None, None),
            P("region", "member", None, None, None),
            P("region", "member", None),
            P("region", "member", None),
            P("region", "member"),
        ),
        out_specs=P("member", "region", None, None),
        check_vma=False,
    )
```

profile of v0, /device:TPU:6, one launch (start us, length us, event | category | flops | bytes accessed | tf_op | source)
XLA Modules:
  0.0 150.1 jit_solution(8650748512281753096)
XLA Ops:
  0.0 2.9 %copy.22 = bf16[16,1,64,512]{3,0,1,2:T(8,128)(2,1)} copy(bf16[16,1,64,512]{3,2,1,0:T(8,128)(2,1)} %param.5) | data formatting | bytes 2097152 | tf_op args[0]
  2.9 22.3 %all-to-all-start = ((bf16[16,1,64,512]{3,0,1,2:T(8,128)(2,1)}), bf16[16,1,64,512]{3,0,1,2:T(8,128)(2,1)S(1)}, u32[]{:S(2)}, u32[]{:S(2)}) async-start(bf16[16,1,64,512]{3,0,1,2:T(8,128)(2,1)} %copy.22), calls=%async_computation | async-start | bytes 2097152 | tf_op jit(solution)/shard_map/all_to_all | solution.py:52
  25.1 0.0 copy-done
  25.2 1.3 collective-permute-start.1
  26.5 3.1 %collective-permute-start = (bf16[1,1,5,128,1024]{4,3,2,1,0:T(8,128)(2,1)S(1)}, bf16[1,1,5,128,1024]{4,3,2,1,0:T(8,128)(2,1)S(1)}, u32[]{:S(2)}, u32[]{:S(2)}) collective-permute-start(bf16[1,1,5,128,1024]{4,3,2,1,0:T(8,128)(2,1)S(1)} %copy-done), channel_id=1, source_target_pairs={{0,1},{1,2},{2,3},{3,4},{4,5},{5,6},{6,7},{7,8},{8,9},{9,10},{10,1... | collective-permute-start | bytes 3932168 | tf_op jit(solution)/shard_map/ppermute | solution.py:19
  30.2 0.0 copy-done.1
  30.3 0.0 collective-permute-done.1
  30.3 1.8 %collective-permute-done = bf16[1,1,5,128,1024]{4,3,2,1,0:T(8,128)(2,1)S(1)} collective-permute-done((bf16[1,1,5,128,1024]{4,3,2,1,0:T(8,128)(2,1)S(1)}, bf16[1,1,5,128,1024]{4,3,2,1,0:T(8,128)(2,1)S(1)}, u32[]{:S(2)}, u32[]{:S(2)}) %collective-permute-start) | collective-permute-done | bytes 1310752 | tf_op jit(solution)/shard_map/ppermute | solution.py:19
  32.1 2.1 %pad_maximum_fusion = bf16[3,1,5,128,1024]{4,3,2,1,0:T(8,128)(2,1)} fusion(bf16[1,1,5,128,1024]{4,3,2,1,0:T(8,128)(2,1)S(1)} %collective-permute-done.1, bf16[1,1,5,128,1024]{4,3,2,1,0:T(8,128)(2,1)S(1)} %copy-done, bf16[1,1,5,128,1024]{4,3,2,1,0:T(8,128)(2,1)S(1)} %collective-permute-done), kind=kLoop, calls=%fused_computation.3 | loop fusion | flops 3932160 | bytes 7864320 | tf_op jit(solution)/shard_map/concatenate | solution.py:17
  34.3 2.7 %gather_fusion = bf16[3,128,1024]{2,1,0:T(8,128)(2,1)S(1)} fusion(bf16[15,128,1024]{2,1,0:T(8,128)(2,1)} %bitcast.30, s32[1024]{0:T(1024)S(1)} %pad_clamp_fusion), kind=kCustom, calls=%fused_computation | custom fusion | bytes 1572876 | tf_op jit(solution)/shard_map/jit(_take)/gather | solution.py:43
  37.0 2.7 %fusion = bf16[1024,1024]{1,0:T(8,128)(2,1)} fusion(bf16[3,128,1024]{2,1,0:T(8,128)(2,1)S(1)} %gather_fusion, pred[3]{0:T(512)(128)(4,1)S(1)} %get-tuple-element.5, pred[3]{0:T(512)(128)(4,1)S(1)} %get-tuple-element.6), kind=kOutput, calls=%fused_computation.2 | convolution fusion | flops 808189952 | bytes 2883590 | tf_op jit(solution)/shard_map/dot_general | solution.py:47
  39.7 40.6 %all-to-all-done = bf16[16,1,64,512]{3,0,1,2:T(8,128)(2,1)S(1)} async-done(((bf16[16,1,64,512]{3,0,1,2:T(8,128)(2,1)}), bf16[16,1,64,512]{3,0,1,2:T(8,128)(2,1)S(1)}, u32[]{:S(2)}, u32[]{:S(2)}) %all-to-all-start) | async-done | bytes 1048608 | tf_op jit(solution)/shard_map/all_to_all | solution.py:52
  80.4 0.6 copy.31
  80.9 0.6 copy.24
  81.5 1.2 convolution_convert_fusion
  82.8 0.3 copy-done.4
  83.1 1.3 fusion.1
  84.4 0.5 broadcast.63
  84.9 1.5 reduce
  86.4 0.8 reshape.70
  87.2 60.0 %all_to_all.33 = bf16[64,2,4096]{2,1,0:T(2,128)(2,1)S(1)} all-to-all(bf16[64,2,4096]{2,1,0:T(2,128)(2,1)S(1)} %reshape.70), channel_id=1, replica_groups=mesh['member'=64,'region'=16] {'member'}, dimensions={0} | all-to-all | bytes 2097152 | tf_op jit(solution)/shard_map/all_to_all | solution.py:54
  147.2 1.0 reshape.71
  148.3 0.3 copy.29
  148.6 1.5 %copy.27 = bf16[16,1,64,512]{3,2,1,0:T(8,128)(2,1)} copy(bf16[16,1,64,512]{3,0,2,1:T(8,128)(2,1)S(1)} %bitcast.31) | data formatting | bytes 2097152 | tf_op jit(solution)/shard_map/all_to_all | solution.py:54
  (10 shorter events, 0.0 us)
Async XLA Ops:
  0.0 25.1 %copy-start = (bf16[1,1,5,128,1024]{4,3,2,1,0:T(8,128)(2,1)S(1)}, bf16[1,1,5,128,1024]{4,3,2,1,0:T(8,128)(2,1)}, u32[]{:S(2)}) copy-start(bf16[1,1,5,128,1024]{4,3,2,1,0:T(8,128)(2,1)} %param.6) | copy-start | bytes 3932164
  0.0 30.2 %copy-start.1 = (s32[1,1,3]{2,1,0:T(1,128)S(1)}, s32[1,1,3]{2,1,0:T(1,128)}, u32[]{:S(2)}) copy-start(s32[1,1,3]{2,1,0:T(1,128)} %param.7) | copy-start | bytes 40
  0.0 30.2 %copy-start.2 = (s32[1,1,3]{2,1,0:T(1,128)S(1)}, s32[1,1,3]{2,1,0:T(1,128)}, u32[]{:S(2)}) copy-start(s32[1,1,3]{2,1,0:T(1,128)} %param.8) | copy-start | bytes 40
  2.9 77.5 %all-to-all-start = ((bf16[16,1,64,512]{3,0,1,2:T(8,128)(2,1)}), bf16[16,1,64,512]{3,0,1,2:T(8,128)(2,1)S(1)}, u32[]{:S(2)}, u32[]{:S(2)}) async-start(bf16[16,1,64,512]{3,0,1,2:T(8,128)(2,1)} %copy.22), calls=%async_computation | async-start | bytes 2097152 | tf_op jit(solution)/shard_map/all_to_all | solution.py:52
  25.2 5.1 %collective-permute-start.1 = (bf16[1,1,5,128,1024]{4,3,2,1,0:T(8,128)(2,1)S(1)}, bf16[1,1,5,128,1024]{4,3,2,1,0:T(8,128)(2,1)S(1)}, u32[]{:S(2)}, u32[]{:S(2)}) collective-permute-start(bf16[1,1,5,128,1024]{4,3,2,1,0:T(8,128)(2,1)S(1)} %copy-done), channel_id=1, source_target_pairs={{1,0},{2,1},{3,2},{4,3},{5,4},{6,5},{7,6},{8,7},{9,8},{10,9},{11,1... | collective-permute-start | bytes 3932168 | tf_op jit(solution)/shard_map/ppermute | solution.py:21
  26.5 5.7 %collective-permute-start = (bf16[1,1,5,128,1024]{4,3,2,1,0:T(8,128)(2,1)S(1)}, bf16[1,1,5,128,1024]{4,3,2,1,0:T(8,128)(2,1)S(1)}, u32[]{:S(2)}, u32[]{:S(2)}) collective-permute-start(bf16[1,1,5,128,1024]{4,3,2,1,0:T(8,128)(2,1)S(1)} %copy-done), channel_id=1, source_target_pairs={{0,1},{1,2},{2,3},{3,4},{4,5},{5,6},{6,7},{7,8},{8,9},{9,10},{10,1... | collective-permute-start | bytes 3932168 | tf_op jit(solution)/shard_map/ppermute | solution.py:19
  39.7 41.8 %copy-start.3 = (bf16[1024,1024]{1,0:T(8,128)(2,1)S(1)}, bf16[1024,1024]{1,0:T(8,128)(2,1)}, u32[]{:S(2)}) copy-start(bf16[1024,1024]{1,0:T(8,128)(2,1)} %fusion) | copy-start | bytes 6291460
  81.5 1.6 %copy-start.4 = (bf16[1024,1024]{1,0:T(8,128)(2,1)S(1)}, bf16[1024,1024]{1,0:T(8,128)(2,1)}, u32[]{:S(2)}) copy-start(bf16[1024,1024]{1,0:T(8,128)(2,1)} %fusion) | copy-start | bytes 6291460
where the time goes:
time: 151 us; the launch traced here: 150 us
  blocking collectives  60 us (40%)
  waiting for transfers between devices  42.5 us (28%)
  starting transfers between devices  26.7 us (18%)
  local copies, waits for them, and re-layouts  11.3 us (7%)
  matrix products  5.25 us (3%)
  other arithmetic  3.6 us (2%)
    all_to_all x1, blocking collectives, shards(): lax.all_to_all(moved, 'member', split_axis=0, concat_axis=2, tiled=True)  60 us
    all_to_all x1, waiting for transfers between devices, shards(): lax.all_to_all(ensemble, 'member', split_axis=2, concat_axis=0, tiled=True)  40.6 us
    all_to_all x1, starting transfers between devices, shards(): lax.all_to_all(ensemble, 'member', split_axis=2, concat_axis=0, tiled=True)  22.3 us
    unnamed x14, local copies, waits for them, and re-layouts  5.35 us
    ppermute x1, starting transfers between devices, padded(): lax.ppermute(tail, axis, [(i, (i + 1) % count) for i in range(ends)])  3.11 us
  transfers between devices with their start and end apart: 3, of which 2 were waited for; matrix products, arithmetic and copies ran while one was open for 5% of the time, Pallas kernels for 0%

commit v1 on v0

v1 whole, which is shorter than its diff:
```python
import functools

import jax
import jax.numpy as jnp
from jax import lax
from jax.experimental import pallas as pl
from jax.experimental.pallas import tpu as pltpu
from jax.sharding import PartitionSpec as P

K = 1024
OBS_DEV = 5
MAXB = 3
CHUNKS = 2
MESH = pl.DeviceIdType.MESH


def kernel(
    nz, nx, nr,
    ids_ref, src_ref, count_ref, ens_hbm, obs_hbm, out_ref,
    ens, packed, xbuf, obuf, rbuf, obs, gram, first,
    ens_sem, obs_sem, obs_send, obs_recv, in_send, in_recv, out_send, out_recv,
):
    me = lax.axis_index("member")
    region = lax.axis_index("region")
    n = nz * nx
    z, x = me // nx, me % nx
    chunks, width = packed.shape[0], packed.shape[3]
    rows = packed.shape[2]
    groups = n // 16

    def peer(i):
        step = i // nx
        dz = nz // 2 + ((step + 1) // 2) * (1 - 2 * (step % 2))
        dx = i % nx + 1
        return ((z + dz + nz) % nz) * nx + (x + dx) % nx

    above, below = (region + 1) % nr, (region + nr - 1) % nr
    barrier = pltpu.get_barrier_semaphore()

    def greet(i, carry):
        pl.semaphore_signal(barrier, inc=1, device_id={"member": peer(i)}, device_id_type=MESH)
        return carry

    lax.fori_loop(0, n - 1, greet, 0)
    for other in (above, below):
        pl.semaphore_signal(barrier, inc=1, device_id={"region": other}, device_id_type=MESH)

    loads = []
    for c in range(chunks):
        cols = pl.ds(c * width, width)
        load = pltpu.make_async_copy(ens_hbm.at[:, 0, :, cols], ens.at[:, :, cols], ens_sem.at[c])
        load.start()
        loads.append(load)
    own_obs = pltpu.make_async_copy(obs_hbm.at[0, 0], obs.at[1], obs_sem)
    own_obs.start()

    i0 = lax.broadcasted_iota(jnp.int32, (256, 256), 0)
    i1 = lax.broadcasted_iota(jnp.int32, (256, 256), 1)
    swap = ((i0 % 16) * 16 + i0 // 16 == i1).astype(jnp.bfloat16)

    def exchange(c):
        return jnp.dot(swap, c, preferred_element_type=jnp.float32).astype(jnp.bfloat16)

    def pack(c):
        for g in range(groups):
            part = ens[:, 16 * g : 16 * g + 16, c * width : (c + 1) * width]
            packed[c, 16 * g : 16 * g + 16] = exchange(part.reshape(256, width)).reshape(16, 16, width)

    def send(c, source, target, send_sem, recv_sem):
        def one(i, carry):
            other = peer(i)
            pltpu.make_async_remote_copy(
                src_ref=source.at[c, other],
                dst_ref=target.at[c, me],
                send_sem=send_sem.at[c],
                recv_sem=recv_sem.at[c],
                device_id={"member": other},
                device_id_type=MESH,
            ).start()
            return carry

        lax.fori_loop(0, n - 1, one, 0)
        target[c, me] = source[c, me]

    def whole(c, source, target, send_sem, recv_sem):
        part = pl.ds(0, n - 1)
        return pltpu.make_async_remote_copy(
            src_ref=source.at[c, part],
            dst_ref=target.at[c, part],
            send_sem=send_sem.at[c],
            recv_sem=recv_sem.at[c],
            device_id={"member": peer(0)},
            device_id_type=MESH,
        )

    incoming = (packed, xbuf, in_send, in_recv)
    outgoing = (obuf, rbuf, out_send, out_recv)

    loads[0].wait()
    pack(0)
    pl.semaphore_wait(barrier, n + 1)
    obs_copies = []
    for slot, other in ((0, above), (2, below)):
        copy = pltpu.make_async_remote_copy(
            src_ref=obs_hbm.at[0, 0],
            dst_ref=obs.at[slot],
            send_sem=obs_send.at[slot // 2],
            recv_sem=obs_recv.at[slot // 2],
            device_id={"region": other},
            device_id_type=MESH,
        )
        copy.start()
        obs_copies.append(copy)
    send(0, *incoming)
    for c in range(1, chunks):
        loads[c].wait()
        pack(c)
        send(c, *incoming)

    own_obs.wait()
    for copy in obs_copies:
        copy.wait()
    blocks = []
    for j in range(MAXB):
        block = obs[src_ref[j], ids_ref[j]]
        blocks.append(jnp.where(j < count_ref[0], block, jnp.zeros((), block.dtype)))
    stacked = jnp.concatenate(blocks, axis=0)
    tile = 256
    for t in range(K // tile):
        full = lax.dot_general(
            stacked[:, t * tile : (t + 1) * tile], stacked, (((0,), (0,)), ((), ())),
            preferred_element_type=jnp.float32,
        )
        gram[t * tile : (t + 1) * tile, :] = (full / (2.0 * K)).astype(jnp.bfloat16)

    for c in range(chunks):
        whole(c, *incoming).wait_recv()

        @pl.loop(0, K // tile)
        def _(t):
            members = xbuf[c].reshape(K, width)
            part = pl.ds(t * tile, tile)
            first[part, :] = jnp.dot(
                gram[part, :], members, preferred_element_type=jnp.float32
            ).astype(jnp.bfloat16)

        @pl.loop(0, K // tile)
        def _(t):
            part = pl.ds(t * tile, tile)
            lots = pl.ds(t * (tile // rows), tile // rows)
            second = jnp.dot(gram[part, :], first[...], preferred_element_type=jnp.float32)
            members = xbuf[c, lots].reshape(tile, width).astype(jnp.float32)
            fresh = members - first[part, :].astype(jnp.float32) + second
            obuf[c, lots] = fresh.astype(jnp.bfloat16).reshape(tile // rows, rows, width)

        send(c, *outgoing)

    for c in range(chunks):
        whole(c, *outgoing).wait_recv()
        for g in range(groups):
            part = rbuf[c, 16 * g : 16 * g + 16].reshape(256, width)
            out_ref[:, 0, 16 * g : 16 * g + 16, c * width : (c + 1) * width] = exchange(part).reshape(16, 16, width)
    for c in range(chunks):
        whole(c, *incoming).wait_send()
        whole(c, *outgoing).wait_send()


def solution(mesh):
    nr = mesh.shape["region"]
    n = mesh.shape["member"]
    nx = 4
    nz = n // nx

    def shards(ensemble, obs_store, block_ids, block_src, block_count):
        rows, _, patches, values = ensemble.shape
        width = values // CHUNKS
        piece = pltpu.VMEM((CHUNKS, n, rows, width), jnp.bfloat16)
        dma = pltpu.SemaphoreType.DMA
        return pl.pallas_call(
            functools.partial(kernel, nz, nx, nr),
            out_shape=jax.ShapeDtypeStruct(ensemble.shape, jnp.bfloat16),
            in_specs=[pl.BlockSpec(memory_space=pltpu.SMEM)] * 3
            + [pl.BlockSpec(memory_space=pl.ANY)] * 2,
            out_specs=pl.BlockSpec(memory_space=pltpu.VMEM),
            scratch_shapes=[
                pltpu.VMEM((rows, patches, values), jnp.bfloat16),
                piece, piece, piece, piece,
                pltpu.VMEM((3,) + obs_store.shape[2:], jnp.bfloat16),
                pltpu.VMEM((K, K), jnp.bfloat16),
                pltpu.VMEM((K, width), jnp.bfloat16),
                dma((CHUNKS,)), dma, dma((2,)), dma((2,)),
                dma((CHUNKS,)), dma((CHUNKS,)), dma((CHUNKS,)), dma((CHUNKS,)),
            ],
            compiler_params=pltpu.CompilerParams(
                collective_id=0, has_side_effects=True, vmem_limit_bytes=62 << 20
            ),
            name="analysis",
        )(
            block_ids.reshape(MAXB), block_src.reshape(MAXB), block_count.reshape(1),
            ensemble, obs_store,
        )

    return jax.shard_map(
        shards,
        mesh=mesh,
        in_specs=(
            P("member", "region", None, None),
            P("region", "member", None, None, None),
            P("region", "member", None),
            P("region", "member", None),
            P("region", "member"),
        ),
        out_specs=P("member", "region", None, None),
        check_vma=False,
    )
```

time: 151 us -> 120 us (0.79)
  Pallas kernels: 0 us -> 115 us
  blocking collectives: 60 us -> 0 us
  waiting for transfers between devices: 42.5 us -> 0 us
  starting transfers between devices: 26.7 us -> 0 us
  local copies, waits for them, and re-layouts: 11.3 us -> 2.29 us
  matrix products: 5.25 us -> 0 us
  other arithmetic: 3.6 us -> 0 us
    pallas_call x0 -> x1, Pallas kernels: none -> 115 us  [shards(): pl.pallas_call(functools.partial(kernel, nz, nx, nr), out_shape=jax.Shape...]
    all_to_all x1 -> x0, blocking collectives: 60 us -> none  [shards(): lax.all_to_all(moved, 'member', split_axis=0, concat_axis=2, tiled=True)]
    all_to_all x1 -> x0, waiting for transfers between devices: 40.6 us -> none  [shards(): lax.all_to_all(ensemble, 'member', split_axis=2, concat_axis=0, tiled=True)]
    all_to_all x1 -> x0, starting transfers between devices: 22.3 us -> none  [shards(): lax.all_to_all(ensemble, 'member', split_axis=2, concat_axis=0, tiled=True)]
    dot_general x3 -> x0, matrix products: 5.25 us -> none  [the longest x1 2.73 us: shards(): lax.dot_general(stacked, stacked, (((0,), (0,)), ((), ())), preferred_ele...]
    ppermute x2 -> x0, starting transfers between devices: 4.41 us -> none  [the longest x1 3.11 us: padded(): lax.ppermute(tail, axis, [(i, (i + 1) % count) for i in range(ends)])]
    unnamed x14 -> x1, local copies, waits for them, and re-layouts: 5.35 us -> 2.29 us
    all_to_all x3 -> x0, local copies, waits for them, and re-layouts: 2.71 us -> none  [the longest x1 1.55 us: shards(): lax.all_to_all(moved, 'member', split_axis=0, concat_axis=2, tiled=True)]
  transfers between devices with their start and end apart: 3 -> 0, of which waited for: 2 -> 0; matrix products, arithmetic and copies ran while one was open for 5% -> 0% of each run, Pallas kernels for 0% -> 0%
where the time goes in v1:
time: 120 us; the launch traced here: 118 us
  Pallas kernels  115 us (96%)
  local copies, waits for them, and re-layouts  2.29 us (2%)
    pallas_call x1, Pallas kernels, shards(): pl.pallas_call(functools.partial(kernel, nz, nx, nr), out_shape=jax.Shape...  115 us

profile of v1, /device:TPU:6, one launch (start us, length us, event | category | flops | bytes accessed | tf_op | source)
XLA Modules:
  0.0 118.0 jit_solution(15452650672282099562)
XLA Ops:
  0.7 115.0 %analysis.1 = bf16[16,1,64,512]{3,2,1,0:T(8,128)(2,1)} custom-call(s32[3]{0:T(128)} %bitcast.4, s32[3]{0:T(128)} %bitcast.5, s32[1]{0:T(128)} %bitcast.3.count_ref, bf16[16,1,64,512]{3,2,1,0:T(8,128)(2,1)} %ens_hbm.1, bf16[1,1,5,128,1024]{4,3,2,1,0:T(8,128)(2,1)} %obs_hbm.1), custom_call_target="tpu_custom_call" | custom-call | tf_op jit(solution)/shard_map/analysis/pallas_call | solution.py:179
  115.7 2.3 %copy.8 = bf16[16,1,64,512]{3,2,1,0:T(8,128)(2,1)} copy(bf16[16,1,64,512]{3,2,1,0:T(8,128)(2,1)} %analysis.1) | data formatting | bytes 2097152

commit v2 on v1

--- a/solution.py
+++ b/solution.py
@@ -16,9 +16,9 @@
 
 def kernel(
     nz, nx, nr,
-    ids_ref, src_ref, count_ref, ens_hbm, obs_hbm, out_ref,
-    ens, packed, xbuf, obuf, rbuf, obs, gram, first,
-    ens_sem, obs_sem, obs_send, obs_recv, in_send, in_recv, out_send, out_recv,
+    ids_hbm, src_hbm, ens_hbm, obs_hbm, count_ref, out_ref,
+    ids_ref, src_ref, ens, packed, xbuf, obuf, rbuf, obs, gram, first,
+    ens_sem, obs_sem, obs_send, obs_recv, in_send, in_recv, out_send, out_recv, int_sem,
 ):
     me = lax.axis_index("member")
     region = lax.axis_index("region")
@@ -53,6 +53,11 @@
         loads.append(load)
     own_obs = pltpu.make_async_copy(obs_hbm.at[0, 0], obs.at[1], obs_sem)
     own_obs.start()
+    ints = []
+    for i, (source, target) in enumerate(((ids_hbm, ids_ref), (src_hbm, src_ref))):
+        load = pltpu.make_async_copy(source, target, int_sem.at[i])
+        load.start()
+        ints.append(load)
 
     i0 = lax.broadcasted_iota(jnp.int32, (256, 256), 0)
     i1 = lax.broadcasted_iota(jnp.int32, (256, 256), 1)
@@ -117,13 +122,15 @@
         pack(c)
         send(c, *incoming)
 
+    for load in ints:
+        load.wait()
     own_obs.wait()
     for copy in obs_copies:
         copy.wait()
     blocks = []
     for j in range(MAXB):
-        block = obs[src_ref[j], ids_ref[j]]
-        blocks.append(jnp.where(j < count_ref[0], block, jnp.zeros((), block.dtype)))
+        block = obs[src_ref[0, 0, j], ids_ref[0, 0, j]]
+        blocks.append(jnp.where(j < count_ref[0, 0], block, jnp.zeros((), block.dtype)))
     stacked = jnp.concatenate(blocks, axis=0)
     tile = 256
     for t in range(K // tile):
@@ -179,25 +186,30 @@
         return pl.pallas_call(
             functools.partial(kernel, nz, nx, nr),
             out_shape=jax.ShapeDtypeStruct(ensemble.shape, jnp.bfloat16),
-            in_specs=[pl.BlockSpec(memory_space=pltpu.SMEM)] * 3
-            + [pl.BlockSpec(memory_space=pl.ANY)] * 2,
+            in_specs=[pl.BlockSpec(memory_space=pltpu.HBM)] * 4
+            + [pl.BlockSpec(memory_space=pltpu.SMEM)],
             out_specs=pl.BlockSpec(memory_space=pltpu.VMEM),
             scratch_shapes=[
+                pltpu.SMEM((1, 1, MAXB), jnp.int32),
+                pltpu.SMEM((1, 1, MAXB), jnp.int32),
                 pltpu.VMEM((rows, patches, values), jnp.bfloat16),
                 piece, piece, piece, piece,
                 pltpu.VMEM((3,) + obs_store.shape[2:], jnp.bfloat16),
                 pltpu.VMEM((K, K), jnp.bfloat16),
                 pltpu.VMEM((K, width), jnp.bfloat16),
                 dma((CHUNKS,)), dma, dma((2,)), dma((2,)),
-                dma((CHUNKS,)), dma((CHUNKS,)), dma((CHUNKS,)), dma((CHUNKS,)),
+                dma((CHUNKS,)), dma((CHUNKS,)), dma((CHUNKS,)), dma((CHUNKS,)), dma((2,)),
             ],
             compiler_params=pltpu.CompilerParams(
-                collective_id=0, has_side_effects=True, vmem_limit_bytes=62 << 20
+                collective_id=0, has_side_effects=True, vmem_limit_bytes=40 << 20
             ),
             name="analysis",
         )(
-            block_ids.reshape(MAXB), block_src.reshape(MAXB), block_count.reshape(1),
-            ensemble, obs_store,
+            *(
+                pltpu.with_memory_space_constraint(value, pltpu.HBM)
+                for value in (block_ids, block_src, ensemble, obs_store)
+            ),
+            block_count,
         )
 
     return jax.shard_map(

time: 120 us -> 117 us (0.975)
  Pallas kernels: 115 us -> 113 us
  local copies, waits for them, and re-layouts: 2.29 us -> 0.97 us
    pallas_call x1, Pallas kernels: 115 us -> 113 us  [shards(): pl.pallas_call(functools.partial(kernel, nz, nx, nr), out_shape=jax.Shape...]
    unnamed x1, local copies, waits for them, and re-layouts: 2.29 us -> 0.97 us
where the time goes in v2:
time: 117 us; the launch traced here: 115 us
  Pallas kernels  113 us (97%)
    pallas_call x1, Pallas kernels, shards(): pl.pallas_call(functools.partial(kernel, nz, nx, nr), out_shape=jax.Shape...  113 us

profile of v2, /device:TPU:6, one launch (start us, length us, event | category | flops | bytes accessed | tf_op | source)
XLA Modules:
  0.0 115.0 jit_solution(1172123403238627043)
XLA Ops:
  0.7 113.4 %analysis.1 = bf16[16,1,64,512]{3,2,1,0:T(8,128)(2,1)S(1)} custom-call(s32[1,1,3]{2,1,0:T(1,128)} %ids_hbm.1, s32[1,1,3]{2,1,0:T(1,128)} %src_hbm.1, bf16[16,1,64,512]{3,2,1,0:T(8,128)(2,1)} %ens_hbm.1, bf16[1,1,5,128,1024]{4,3,2,1,0:T(8,128)(2,1)} %obs_hbm.1, s32[1,1]{1,0:T(1,128)S(6)} %copy.7.count_ref), custom_call_target="tpu_custom_call" | custom-call | tf_op jit(solution)/shard_map/analysis/pallas_call | solution.py:186
  114.1 1.0 copy.8

commit v3 on v2

--- a/solution.py
+++ b/solution.py
@@ -19,6 +19,7 @@
     ids_hbm, src_hbm, ens_hbm, obs_hbm, count_ref, out_ref,
     ids_ref, src_ref, ens, packed, xbuf, obuf, rbuf, obs, gram, first,
     ens_sem, obs_sem, obs_send, obs_recv, in_send, in_recv, out_send, out_recv, int_sem,
+    chain, arrived,
 ):
     me = lax.axis_index("member")
     region = lax.axis_index("region")
@@ -28,22 +29,25 @@
     rows = packed.shape[2]
     groups = n // 16
 
-    def peer(i):
-        step = i // nx
-        dz = nz // 2 + ((step + 1) // 2) * (1 - 2 * (step % 2))
-        dx = i % nx + 1
-        return ((z + dz + nz) % nz) * nx + (x + dx) % nx
-
     above, below = (region + 1) % nr, (region + nr - 1) % nr
     barrier = pltpu.get_barrier_semaphore()
 
-    def greet(i, carry):
-        pl.semaphore_signal(barrier, inc=1, device_id={"member": peer(i)}, device_id_type=MESH)
-        return carry
-
-    lax.fori_loop(0, n - 1, greet, 0)
+    def greet(device):
+        pl.semaphore_signal(barrier, inc=1, device_id=device, device_id_type=MESH)
+
+    for dx in range(1, nx):
+        greet({"member": z * nx + (x + dx) % nx})
+
+    @pl.when(z > 0)
+    def _():
+        greet({"member": me - nx})
+
+    @pl.when(z < nz - 1)
+    def _():
+        greet({"member": me + nx})
+
     for other in (above, below):
-        pl.semaphore_signal(barrier, inc=1, device_id={"region": other}, device_id_type=MESH)
+        greet({"region": other})
 
     loads = []
     for c in range(chunks):
@@ -71,21 +75,33 @@
             part = ens[:, 16 * g : 16 * g + 16, c * width : (c + 1) * width]
             packed[c, 16 * g : 16 * g + 16] = exchange(part.reshape(256, width)).reshape(16, 16, width)
 
-    def send(c, source, target, send_sem, recv_sem):
-        def one(i, carry):
-            other = peer(i)
-            pltpu.make_async_remote_copy(
-                src_ref=source.at[c, other],
-                dst_ref=target.at[c, me],
-                send_sem=send_sem.at[c],
-                recv_sem=recv_sem.at[c],
-                device_id={"member": other},
-                device_id_type=MESH,
-            ).start()
+    def send_row(c, row, source, target, send_sem, recv_sem):
+        for dx in range(nx):
+            other = row * nx + (x + dx) % nx
+
+            def start(other=other):
+                pltpu.make_async_remote_copy(
+                    src_ref=source.at[c, other],
+                    dst_ref=target.at[c, me],
+                    send_sem=send_sem.at[c],
+                    recv_sem=recv_sem.at[c],
+                    device_id={"member": other},
+                    device_id_type=MESH,
+                ).start()
+
+            if dx == 0:
+                pl.when(row != z)(start)
+            else:
+                start()
+
+    def far_first(chosen, c, source, target, send_sem, recv_sem):
+        def one(step, carry):
+            dz = nz // 2 + ((step + 1) // 2) * (1 - 2 * (step % 2))
+            row = (z + dz + nz) % nz
+            pl.when(chosen(row))(lambda: send_row(c, row, source, target, send_sem, recv_sem))
             return carry
 
-        lax.fori_loop(0, n - 1, one, 0)
-        target[c, me] = source[c, me]
+        lax.fori_loop(0, nz, one, 0)
 
     def whole(c, source, target, send_sem, recv_sem):
         part = pl.ds(0, n - 1)
@@ -94,16 +110,34 @@
             dst_ref=target.at[c, part],
             send_sem=send_sem.at[c],
             recv_sem=recv_sem.at[c],
-            device_id={"member": peer(0)},
+            device_id={"member": (me + 1) % n},
             device_id_type=MESH,
         )
 
     incoming = (packed, xbuf, in_send, in_recv)
     outgoing = (obuf, rbuf, out_send, out_recv)
 
-    loads[0].wait()
-    pack(0)
-    pl.semaphore_wait(barrier, n + 1)
+    for c in range(chunks):
+        loads[c].wait()
+        pack(c)
+        xbuf[c, me] = packed[c, me]
+    inner = jnp.where(z > 0, 1, 0) + jnp.where(z < nz - 1, 1, 0)
+    pl.semaphore_wait(barrier, nx + 1 + inner)
+
+    @pl.when(z > 0)
+    def _():
+        pl.semaphore_wait(chain, 1)
+
+    @pl.when(z < nz - 1)
+    def _():
+        pl.semaphore_signal(chain, inc=1, device_id={"member": me + nx}, device_id_type=MESH)
+
+    def arrive(i, carry):
+        pl.semaphore_signal(arrived.at[z], inc=1, device_id={"member": i}, device_id_type=MESH)
+        return carry
+
+    lax.fori_loop(0, z * nx, arrive, 0)
+
     obs_copies = []
     for slot, other in ((0, above), (2, below)):
         copy = pltpu.make_async_remote_copy(
@@ -116,11 +150,16 @@
         )
         copy.start()
         obs_copies.append(copy)
-    send(0, *incoming)
+    far_first(lambda row: row <= z, 0, *incoming)
+
+    def fresh_row(row, carry):
+        pl.semaphore_wait(arrived.at[row], nx)
+        send_row(0, row, *incoming)
+        return carry
+
+    lax.fori_loop(z + 1, nz, fresh_row, 0)
     for c in range(1, chunks):
-        loads[c].wait()
-        pack(c)
-        send(c, *incoming)
+        far_first(lambda row: row >= 0, c, *incoming)
 
     for load in ints:
         load.wait()
@@ -160,7 +199,13 @@
             fresh = members - first[part, :].astype(jnp.float32) + second
             obuf[c, lots] = fresh.astype(jnp.bfloat16).reshape(tile // rows, rows, width)
 
-        send(c, *outgoing)
+        rbuf[c, me] = obuf[c, me]
+        if c < chunks - 1:
+            far_first(lambda row: row >= 0, c, *outgoing)
+        else:
+            half = nz // 2
+            far_first(lambda row: (row < half) | (z < half), c, *outgoing)
+            far_first(lambda row: (row >= half) & (z >= half), c, *outgoing)
 
     for c in range(chunks):
         whole(c, *outgoing).wait_recv()
@@ -199,6 +244,7 @@
                 pltpu.VMEM((K, width), jnp.bfloat16),
                 dma((CHUNKS,)), dma, dma((2,)), dma((2,)),
                 dma((CHUNKS,)), dma((CHUNKS,)), dma((CHUNKS,)), dma((CHUNKS,)), dma((2,)),
+                pltpu.SemaphoreType.REGULAR, pltpu.SemaphoreType.REGULAR((nz,)),
             ],
             compiler_params=pltpu.CompilerParams(
                 collective_id=0, has_side_effects=True, vmem_limit_bytes=40 << 20

time: 117 us -> 120 us (1.026); the launches traced: 115 us -> 120 us
  Pallas kernels: 113 us -> 118 us
    pallas_call x1, Pallas kernels: 113 us -> 118 us  [shards(): pl.pallas_call(functools.partial(kernel, nz, nx, nr), out_shape=jax.Shape...]
where the time goes in v3:
time: 120 us
  Pallas kernels  118 us (98%)
    pallas_call x1, Pallas kernels, shards(): pl.pallas_call(functools.partial(kernel, nz, nx, nr), out_shape=jax.Shape...  118 us

profile of v3, /device:TPU:6, one launch (start us, length us, event | category | flops | bytes accessed | tf_op | source)
XLA Modules:
  0.0 119.5 jit_solution(3584495733526575122)
XLA Ops:
  0.7 117.9 %analysis.1 = bf16[16,1,64,512]{3,2,1,0:T(8,128)(2,1)S(1)} custom-call(s32[1,1,3]{2,1,0:T(1,128)} %ids_hbm.1, s32[1,1,3]{2,1,0:T(1,128)} %src_hbm.1, bf16[16,1,64,512]{3,2,1,0:T(8,128)(2,1)} %ens_hbm.1, bf16[1,1,5,128,1024]{4,3,2,1,0:T(8,128)(2,1)} %obs_hbm.1, s32[1,1]{1,0:T(1,128)S(6)} %copy.7.count_ref), custom_call_target="tpu_custom_call" | custom-call | tf_op jit(solution)/shard_map/analysis/pallas_call | solution.py:231
  118.5 1.0 copy.8

commit v4 on v3

--- a/solution.py
+++ b/solution.py
@@ -30,6 +30,17 @@
     groups = n // 16
 
     above, below = (region + 1) % nr, (region + nr - 1) % nr
+    late = 11
+    special = (region <= 1) | (region == nr - 1)
+
+    def place(row):
+        return jnp.where(special, jnp.where(row == 0, late, jnp.where(row <= late, row - 1, row)), row)
+
+    def row_at(pos):
+        return jnp.where(special, jnp.where(pos == late, 0, jnp.where(pos < late, pos + 1, pos)), pos)
+
+    pos = place(z)
+    ahead, behind = row_at(pos + 1) * nx + x, row_at(pos - 1) * nx + x
     barrier = pltpu.get_barrier_semaphore()
 
     def greet(device):
@@ -38,13 +49,13 @@
     for dx in range(1, nx):
         greet({"member": z * nx + (x + dx) % nx})
 
-    @pl.when(z > 0)
-    def _():
-        greet({"member": me - nx})
-
-    @pl.when(z < nz - 1)
-    def _():
-        greet({"member": me + nx})
+    @pl.when(pos > 0)
+    def _():
+        greet({"member": behind})
+
+    @pl.when(pos < nz - 1)
+    def _():
+        greet({"member": ahead})
 
     for other in (above, below):
         greet({"region": other})
@@ -121,22 +132,22 @@
         loads[c].wait()
         pack(c)
         xbuf[c, me] = packed[c, me]
-    inner = jnp.where(z > 0, 1, 0) + jnp.where(z < nz - 1, 1, 0)
+    inner = jnp.where(pos > 0, 1, 0) + jnp.where(pos < nz - 1, 1, 0)
     pl.semaphore_wait(barrier, nx + 1 + inner)
 
-    @pl.when(z > 0)
+    @pl.when(pos > 0)
     def _():
         pl.semaphore_wait(chain, 1)
 
-    @pl.when(z < nz - 1)
-    def _():
-        pl.semaphore_signal(chain, inc=1, device_id={"member": me + nx}, device_id_type=MESH)
+    @pl.when(pos < nz - 1)
+    def _():
+        pl.semaphore_signal(chain, inc=1, device_id={"member": ahead}, device_id_type=MESH)
 
     def arrive(i, carry):
-        pl.semaphore_signal(arrived.at[z], inc=1, device_id={"member": i}, device_id_type=MESH)
+        pl.semaphore_signal(arrived.at[z], inc=1, device_id={"member": row_at(i // nx) * nx + i % nx}, device_id_type=MESH)
         return carry
 
-    lax.fori_loop(0, z * nx, arrive, 0)
+    lax.fori_loop(0, pos * nx, arrive, 0)
 
     obs_copies = []
     for slot, other in ((0, above), (2, below)):
@@ -150,14 +161,15 @@
         )
         copy.start()
         obs_copies.append(copy)
-    far_first(lambda row: row <= z, 0, *incoming)
-
-    def fresh_row(row, carry):
+    far_first(lambda row: place(row) <= pos, 0, *incoming)
+
+    def fresh_row(p, carry):
+        row = row_at(p)
         pl.semaphore_wait(arrived.at[row], nx)
         send_row(0, row, *incoming)
         return carry
 
-    lax.fori_loop(z + 1, nz, fresh_row, 0)
+    lax.fori_loop(pos + 1, nz, fresh_row, 0)
     for c in range(1, chunks):
         far_first(lambda row: row >= 0, c, *incoming)
 

time: 120 us -> 121 us (level); the launches traced: 120 us -> 119 us
  no operation moved by 1% of the time
where the time goes in v4:
time: 121 us; the launch traced here: 119 us
  Pallas kernels  117 us (97%)
    pallas_call x1, Pallas kernels, shards(): pl.pallas_call(functools.partial(kernel, nz, nx, nr), out_shape=jax.Shape...  117 us

profile of v4, /device:TPU:6, one launch (start us, length us, event | category | flops | bytes accessed | tf_op | source)
XLA Modules:
  0.0 118.6 jit_solution(13886937950653229004)
XLA Ops:
  0.7 117.0 %analysis.1 = bf16[16,1,64,512]{3,2,1,0:T(8,128)(2,1)S(1)} custom-call(s32[1,1,3]{2,1,0:T(1,128)} %ids_hbm.1, s32[1,1,3]{2,1,0:T(1,128)} %src_hbm.1, bf16[16,1,64,512]{3,2,1,0:T(8,128)(2,1)} %ens_hbm.1, bf16[1,1,5,128,1024]{4,3,2,1,0:T(8,128)(2,1)} %obs_hbm.1, s32[1,1]{1,0:T(1,128)S(6)} %copy.7.count_ref), custom_call_target="tpu_custom_call" | custom-call | tf_op jit(solution)/shard_map/analysis/pallas_call | solution.py:243
  117.6 1.0 copy.8
